TPU v7x, 32 devices: a whole 2x2x4 slice. The times are simulated.
32 devices in a mesh: row: 8 (over z, y), col: 4 (over x, core).
Axes of the slice: x: 2, y: 2, z: 4, core: 2. Of those that a mesh axis runs over, the one named last changes fastest.
Arguments:
- ancestor_inverse: float32 [12288, 12288], P('row', 'col'), may hold values from -5 to 320, as said below
- panel_one: float32 [12288, 256], P(('row', 'col')), may hold values from -0.015625 to 0.015625
- struct_one: int32 [10752], replicated, may hold values from 0 to 12287, as said below
- lower_one: float32 [256, 256], replicated, may hold values from -1 to 2, as said below
- panel_two: float32 [12288, 256], P(('row', 'col')), may hold values from -0.015625 to 0.015625
- struct_two: int32 [9216], replicated, may hold values from 0 to 12287, as said below
- panel_above: float32 [256, 256], replicated, may hold values from -0.375 to 0.375
- lower_two: float32 [256, 256], replicated, may hold values from -1 to 2, as said below
- tile_owner: int32 [192, 1], P(('col', 'row')), may hold values from 0 to 3; in each aligned block of 6 rows (0 to 5, 6 to 11, ...) at most 2 rows name the same one
Outputs:
- inverse_one: float32 [12288, 256], P(('col', 'row'))
- diag_one: float32 [256, 256], replicated
- cross_two: float32 [256, 256], replicated
- diag_two: float32 [256, 256], replicated
- delivered: float32 [256, 64, 256], P(('row', 'col'))
Inputs may be any that keep to these rules, and one draw needn't show every extreme that they name: ancestor_inverse is exactly symmetric and positive definite. `struct_one`: 10752 distinct row numbers of the ancestor block. `struct_two`: 9216 distinct entries of struct_one. `lower_one`: lower triangular with a positive diagonal. `lower_two`: lower triangular with a positive diagonal. `tile_owner`: within each aligned block of 6 entries (the tiles of one device) no value appears more than 2 times; in some block a value appears exactly 2 times.
All inputs are finite; a program needn't handle non-finite values.
Results may differ from a plain program's by a relative error of at most 0.00007.
Values sent between devices are 32-bit elements; how exact they have to be, the bound alone decides.
A program may use at most 64 MiB of HBM per device.

v0:
```python
import jax
import jax.numpy as jnp
from jax import lax
from jax.sharding import PartitionSpec as P

CAP = 2


def matmul(left, right):
    return jnp.dot(left, right, precision=lax.Precision.HIGHEST, preferred_element_type=jnp.float32)


def contract_rows(left, right, precision=lax.Precision.HIGHEST):
    return lax.dot_general(
        left,
        right,
        (((0,), (0,)), ((), ())),
        precision=precision,
        preferred_element_type=jnp.float32,
    )


def row_mask(struct, count):
    lanes = 128
    high = struct // lanes
    low = struct % lanes
    high_hot = (jnp.arange(count // lanes, dtype=jnp.int32)[:, None] == high[None, :]).astype(
        jnp.bfloat16
    )
    low_hot = (jnp.arange(lanes, dtype=jnp.int32)[:, None] == low[None, :]).astype(jnp.bfloat16)
    counts = lax.dot_general(
        high_hot, low_hot, (((1,), (1,)), ((), ())), preferred_element_type=jnp.float32
    )
    return (counts > 0.5).astype(jnp.float32).reshape(count)


def deliver(values, tile_owner, col_count):
    tile_count = tile_owner.shape[0]
    tile_rows = values.shape[0] // tile_count
    all_tiles = values.reshape(tile_count, tile_rows, values.shape[1])
    owner_col = tile_owner[:, 0]
    col_ids = jnp.arange(col_count, dtype=jnp.int32)
    onehot = (owner_col[:, None] == col_ids[None, :]).astype(jnp.int32)
    tile_rank = jnp.sum((jnp.cumsum(onehot, axis=0) - onehot) * onehot, axis=1)
    slot_index = jnp.arange(CAP, dtype=jnp.int32)
    select = (
        (owner_col[None, None, :] == col_ids[:, None, None])
        & (tile_rank[None, None, :] == slot_index[None, :, None])
    ).astype(jnp.float32)
    outgoing = jnp.einsum("cks,srb->ckrb", select, all_tiles, precision=lax.Precision.HIGHEST)
    incoming = lax.all_to_all(outgoing, "col", split_axis=0, concat_axis=0, tiled=True)
    return incoming.reshape(col_count * CAP, tile_rows, values.shape[1])


def local(
    ancestor_inverse,
    panel_one,
    struct_one,
    lower_one,
    panel_two,
    struct_two,
    panel_above,
    lower_two,
    tile_owner,
):
    row_count = lax.axis_size("row")
    col_count = lax.axis_size("col")
    row_index = lax.axis_index("row")
    col_index = lax.axis_index("col")
    local_rows = panel_one.shape[0]
    order = local_rows * row_count * col_count
    width = panel_one.shape[1]
    mask_one = row_mask(struct_one, order)
    mask_two = row_mask(struct_two, order)
    panel_start = (row_index * col_count + col_index) * local_rows
    result_start = (col_index * row_count + row_index) * local_rows
    local_one = panel_one * lax.dynamic_slice_in_dim(mask_one, panel_start, local_rows)[:, None]
    local_two = panel_two * lax.dynamic_slice_in_dim(mask_two, panel_start, local_rows)[:, None]
    result_mask_one = lax.dynamic_slice_in_dim(mask_one, result_start, local_rows)[:, None]
    result_mask_two = lax.dynamic_slice_in_dim(mask_two, result_start, local_rows)[:, None]
    both = jnp.concatenate([local_one, local_two], axis=1)
    gathered = lax.all_gather(both, "col", axis=0, tiled=True)
    moves = [(f, f % row_count * col_count + f // row_count) for f in range(row_count * col_count)]
    resident = lax.ppermute(both, ("row", "col"), moves)
    product = lax.psum_scatter(
        contract_rows(ancestor_inverse, gathered, lax.Precision.HIGH),
        "row",
        scatter_dimension=0,
        tiled=True,
    )
    resident_one = resident[:, :width]
    resident_two = resident[:, width:]
    inverse_one = -product[:, :width] * result_mask_one
    inverse_two = -(product[:, width:] + matmul(inverse_one, panel_above)) * result_mask_two
    sums = lax.psum(
        jnp.concatenate(
            [
                contract_rows(resident_one, inverse_one),
                contract_rows(inverse_one, resident_two),
                contract_rows(resident_two, inverse_two),
            ],
            axis=1,
        ),
        ("row", "col"),
    )
    gram_one = sums[:, :width]
    cross_sum = sums[:, width : 2 * width]
    gram_two = sums[:, 2 * width :]
    diag_one = matmul(lower_one.T, lower_one) - gram_one
    cross_two = -(cross_sum + matmul(diag_one, panel_above))
    diag_two = matmul(lower_two.T, lower_two) - gram_two - matmul(panel_above.T, cross_two)
    delivered = deliver(inverse_two, tile_owner, col_count)
    return (inverse_one, diag_one, cross_two, diag_two, delivered)


def solution(mesh):
    return jax.shard_map(
        local,
        mesh=mesh,
        in_specs=(
            P("row", "col"),
            P(("row", "col"), None),
            P(),
            P(),
            P(("row", "col"), None),
            P(),
            P(),
            P(),
            P(("col", "row"), None),
        ),
        out_specs=(P(("col", "row"), None), P(), P(), P(), P(("row", "col"), None, None)),
        check_vma=False,
    )
```

profile of v0, /device:TPU:0, one launch (start us, length us, event | category | flops | bytes accessed | tf_op | source)
XLA Modules:
  0.0 391.7 jit_solution(2987590773812136722)
XLA Ops:
  7.3 0.9 add_select_fusion.1
  8.2 0.8 add_select_fusion.3
  9.0 1.4 fusion.15
  10.4 1.3 fusion.12
  12.0 1.0 pad_maximum_fusion
  13.1 31.3 %all-gather.2.cloned.1.call-done = f32[1536,512]{1,0:T(8,128)} async-done(((f32[384,512]{1,0:T(8,128)}), f32[1536,512]{1,0:T(8,128)}) %all-gather.2.cloned.1.call-update) | async-done | bytes 3145744 | tf_op jit(solution)/shard_map/all_gather | solution.py:82
  44.4 22.2 %convolution_bitcast_fusion = f32[3072,512]{0,1:T(8,128)} fusion(f32[1536,512]{1,0:T(8,128)} %all-gather.2.cloned.1.call-done, f32[1536,3072]{1,0:T(8,128)} %param.9), kind=kOutput, calls=%fused_computation.2 | convolution fusion | flops 14495514624 | bytes 28311552 | tf_op jit(solution)/shard_map/dot_general | solution.py:14
  66.6 1.1 copy-done.1
  68.7 166.1 %reduce-scatter.2.cloned.1.call-done = f32[384,512]{0,1:T(8,128)} async-done(((f32[3072,512]{0,1:T(8,128)}), f32[384,512]{0,1:T(8,128)}) %reduce-scatter.2.cloned.1.call-update) | async-done | bytes 786448 | tf_op jit(solution)/shard_map/reduce_scatter | solution.py:85
  234.8 1.0 fusion.21
  235.9 1.6 fusion.7
  238.4 0.9 copy.46
  239.2 3.5 all-to-all-start
  243.0 0.8 fusion.19
  244.4 0.8 fusion.22
  245.2 1.0 pad_maximum_fusion.1
  246.2 0.9 copy.47
  247.1 4.4 %all-to-all-done = f32[4,2,64,256]{3,2,1,0:T(8,128)S(1)} async-done(((f32[4,2,64,256]{3,2,1,0:T(8,128)}), f32[4,2,64,256]{3,2,1,0:T(8,128)S(1)}, u32[]{:S(2)}, u32[]{:S(2)}) %all-to-all-start) | async-done | bytes 524320 | tf_op jit(solution)/shard_map/all_to_all | solution.py:51
  251.5 126.9 %all-reduce.2.cloned.1.call-done = f32[256,768]{1,0:T(8,128)} async-done(((f32[256,768]{1,0:T(8,128)}), f32[256,768]{1,0:T(8,128)}) %all-reduce.2.cloned.1.call-update) | async-done | bytes 786448 | tf_op jit(solution)/shard_map/psum | solution.py:95
  378.4 1.5 convolution_subtract_fusion.1
  379.9 1.4 fusion.9
  381.4 1.6 convolution_subtract_fusion
  383.0 1.3 fusion.8
  384.3 0.8 copy.60
  (36 shorter events, 3.1 us)
Async XLA Ops:
  7.2 228.7 %copy-start = (f32[256,256]{1,0:T(8,128)S(1)}, f32[256,256]{1,0:T(8,128)}, u32[]{:S(2)}) copy-start(f32[256,256]{1,0:T(8,128)} %param.15) | copy-start | bytes 786436
  7.2 4.6 %copy-start.6 = (f32[384,256]{1,0:T(8,128)S(1)}, f32[384,256]{1,0:T(8,128)}, u32[]{:S(2)}) copy-start(f32[384,256]{1,0:T(8,128)} %param.13) | copy-start | bytes 1179652
  7.2 4.7 %copy-start.7 = (f32[384,256]{1,0:T(8,128)S(1)}, f32[384,256]{1,0:T(8,128)}, u32[]{:S(2)}) copy-start(f32[384,256]{1,0:T(8,128)} %param.10) | copy-start | bytes 1179652
  7.2 37.2 %all-gather.2.cloned.1.call-start = ((), (), s32[]{:S(2)}) async-start(), calls=%async_computation.2 | async-start | bytes 3932160 | tf_op jit(solution)/shard_map/all_gather | solution.py:82
  13.0 221.8 %reduce-scatter.2.cloned.1.call-start = ((), (), s32[]{:S(2)}) async-start(), calls=%async_computation.3 | async-start | bytes 7077888 | tf_op jit(solution)/shard_map/reduce_scatter | solution.py:85
  66.6 1.1 copy-start.1
  66.6 1.8 copy-start.8
  67.7 175.2 %collective-permute-start = (f32[384,512]{1,0:T(8,128)S(1)}, f32[384,512]{1,0:T(8,128)S(1)}, u32[]{:S(2)}, u32[]{:S(2)}) collective-permute-start(f32[384,512]{1,0:T(8,128)S(1)} %copy-done.1), channel_id=1, source_target_pairs={{0,0},{1,4},{2,8},{3,12},{4,16},{5,20},{6,24},{7,28},{8,1},{9,5},{... | collective-permute-start | bytes 2359304 | tf_op jit(solution)/shard_map/ppermute | solution.py:84
  238.3 140.0 %copy-start.2 = (f32[256,256]{1,0:T(8,128)S(1)}, f32[256,256]{1,0:T(8,128)}, u32[]{:S(2)}) copy-start(f32[256,256]{1,0:T(8,128)} %param.12) | copy-start | bytes 786436
  239.2 12.3 %all-to-all-start = ((f32[4,2,64,256]{3,2,1,0:T(8,128)}), f32[4,2,64,256]{3,2,1,0:T(8,128)S(1)}, u32[]{:S(2)}, u32[]{:S(2)}) async-start(f32[4,2,64,256]{3,2,1,0:T(8,128)} %copy.46), calls=%async_computation.1 | async-start | bytes 1048576 | tf_op jit(solution)/shard_map/all_to_all | solution.py:51
  242.7 135.6 %all-reduce.2.cloned.1.call-start = ((), (), s32[]{:S(2)}) async-start(), calls=%async_computation.4 | async-start | bytes 1572864 | tf_op jit(solution)/shard_map/psum | solution.py:95
  243.0 138.4 %copy-start.3 = (f32[256,256]{1,0:T(8,128)S(1)}, f32[256,256]{1,0:T(8,128)}, u32[]{:S(2)}) copy-start(f32[256,256]{1,0:T(8,128)} %param.16) | copy-start | bytes 786436
  379.9 5.2 %copy-start.4 = (f32[256,256]{1,0:T(8,128)}, f32[256,256]{1,0:T(8,128)S(1)}, u32[]{:S(2)}) copy-start(f32[256,256]{1,0:T(8,128)S(1)} %convolution_subtract_fusion.1) | copy-start | bytes 786436
  381.4 3.8 copy-start.5
Sparse Core Ops, SparseCore 0:
  13.2 31.2 all-gather.1
  66.7 168.0 reduce-scatter.1
  248.7 129.5 all-reduce.1
where the time goes:
time: 392 us
  waiting for transfers between devices  329 us (84%)
  matrix products  35.3 us (9%)
  between operations  14 us (4%)
  other arithmetic  5.13 us (1%)
  starting transfers between devices  4.47 us (1%)
  local copies, waits for them, and re-layouts  4 us (1%)
    reduce_scatter x1, waiting for transfers between devices, local(): lax.psum_scatter(contract_rows(ancestor_inverse, gathered, lax.Precision....  166 us
    psum x1, waiting for transfers between devices, local(): lax.psum(jnp.concatenate([contract_rows(resident_one, inverse_one), contr...  127 us
    all_gather x1, waiting for transfers between devices, local(): gathered = lax.all_gather(both, 'col', axis=0, tiled=True)  31.3 us
    dot_general x4, matrix products, contract_rows(): lax.dot_general(left, right, (((0,), (0,)), ((), ())), precision=precisio...  24.4 us
  transfers between devices with their start and end apart: 5, of which 4 were waited for; matrix products, arithmetic and copies ran while one was open for 2% of the time, Pallas kernels for 0%

commit v1 on v0

--- a/solution.py
+++ b/solution.py
@@ -4,6 +4,11 @@
 from jax.sharding import PartitionSpec as P
 
 CAP = 2
+
+
+def summed_here(x, axis):
+    blocks = lax.all_gather(x, axis)
+    return jnp.sum(blocks, axis=0)
 
 
 def matmul(left, right):
@@ -92,7 +97,7 @@
     resident_two = resident[:, width:]
     inverse_one = -product[:, :width] * result_mask_one
     inverse_two = -(product[:, width:] + matmul(inverse_one, panel_above)) * result_mask_two
-    sums = lax.psum(
+    sums = summed_here(
         jnp.concatenate(
             [
                 contract_rows(resident_one, inverse_one),

time: 392 us -> 446 us (1.14)
  waiting for transfers between devices: 329 us -> 364 us
  local copies, waits for them, and re-layouts: 4 us -> 19.6 us
  other arithmetic: 5.13 us -> 11 us
    all_gather x0 -> x1, waiting for transfers between devices: none -> 155 us  [summed_here(): blocks = lax.all_gather(x, axis)]
    psum x1 -> x0, waiting for transfers between devices: 127 us -> none  [local(): lax.psum(jnp.concatenate([contract_rows(resident_one, inverse_one), contr...]
    unnamed x20 -> x24, local copies, waits for them, and re-layouts: 2.86 us -> 18.4 us
    all_to_all x1, waiting for transfers between devices: 4.39 us -> 11.7 us  [deliver(): lax.all_to_all(outgoing, 'col', split_axis=0, concat_axis=0, tiled=True)]
    reduce_sum x0 -> x1, other arithmetic: none -> 5.83 us  [summed_here(): return jnp.sum(blocks, axis=0)]
  transfers between devices with their start and end apart: 5 -> 5, of which waited for: 4 -> 4; matrix products, arithmetic and copies ran while one was open for 2% -> 1% of each run, Pallas kernels for 0% -> 0%
where the time goes in v1:
time: 446 us; the launch traced here: 445 us
  waiting for transfers between devices  364 us (82%)
  matrix products  32 us (7%)
  local copies, waits for them, and re-layouts  19.6 us (4%)
  between operations  14.1 us (3%)
  other arithmetic  11 us (2%)
  starting transfers between devices  4.47 us (1%)
    reduce_scatter x1, waiting for transfers between devices, local(): lax.psum_scatter(contract_rows(ancestor_inverse, gathered, lax.Precision....  166 us
    all_gather x1, waiting for transfers between devices, summed_here(): blocks = lax.all_gather(x, axis)  155 us
    all_gather x1, waiting for transfers between devices, local(): gathered = lax.all_gather(both, 'col', axis=0, tiled=True)  31.3 us
    dot_general x4, matrix products, contract_rows(): lax.dot_general(left, right, (((0,), (0,)), ((), ())), precision=precisio...  24.1 us
    unnamed x24, local copies, waits for them, and re-layouts  18.4 us
    all_to_all x1, waiting for transfers between devices, deliver(): lax.all_to_all(outgoing, 'col', split_axis=0, concat_axis=0, tiled=True)  11.7 us
  transfers between devices with their start and end apart: 5, of which 4 were waited for; matrix products, arithmetic and copies ran while one was open for 1% of the time, Pallas kernels for 0%

profile of v1, /device:TPU:0, one launch (start us, length us, event | category | flops | bytes accessed | tf_op | source)
XLA Modules:
  0.0 445.2 jit_solution(14361510297091302747)
XLA Ops:
  7.3 0.9 add_select_fusion.1
  8.2 0.8 add_select_fusion.3
  9.0 1.4 fusion.15
  10.4 1.3 fusion.12
  12.0 1.0 pad_maximum_fusion
  13.1 31.3 %all-gather.4.cloned.1.call-done = f32[1536,512]{1,0:T(8,128)} async-done(((f32[384,512]{1,0:T(8,128)}), f32[1536,512]{1,0:T(8,128)}) %all-gather.4.cloned.1.call-update) | async-done | bytes 3145744 | tf_op jit(solution)/shard_map/all_gather | solution.py:87
  44.4 22.1 %convolution_bitcast_fusion = f32[3072,512]{0,1:T(8,128)} fusion(f32[1536,512]{1,0:T(8,128)} %all-gather.4.cloned.1.call-done, f32[1536,3072]{1,0:T(8,128)} %param.9), kind=kOutput, calls=%fused_computation.3 | convolution fusion | flops 14495514624 | bytes 28311552 | tf_op jit(solution)/shard_map/dot_general | solution.py:19
  66.6 1.0 copy-done.1
  67.7 0.7 collective-permute-start
  68.4 166.4 %reduce-scatter.2.cloned.1.call-done = f32[384,512]{0,1:T(8,128)} async-done(((f32[3072,512]{0,1:T(8,128)}), f32[384,512]{0,1:T(8,128)}) %reduce-scatter.2.cloned.1.call-update) | async-done | bytes 786448 | tf_op jit(solution)/shard_map/reduce_scatter | solution.py:90
  234.8 1.0 fusion.21
  236.4 0.8 fusion.24
  237.2 1.6 fusion.7
  239.5 1.0 pad_maximum_fusion.1
  240.9 0.7 fusion.16
  241.6 0.9 copy.40
  242.5 3.7 all-to-all-start
  246.2 0.9 copy.41
  247.1 11.7 %all-to-all-done = f32[4,2,64,256]{3,2,1,0:T(8,128)S(1)} async-done(((f32[4,2,64,256]{3,2,1,0:T(8,128)}), f32[4,2,64,256]{3,2,1,0:T(8,128)S(1)}, u32[]{:S(2)}, u32[]{:S(2)}) %all-to-all-start) | async-done | bytes 524320 | tf_op jit(solution)/shard_map/all_to_all | solution.py:56
  258.8 154.6 %all-gather.6.cloned.1.call-done = f32[8192,768]{0,1:T(8,128)} async-done(((f32[256,768]{0,1:T(8,128)}), f32[8192,768]{0,1:T(8,128)}) %all-gather.6.cloned.1.call-update) | async-done | bytes 25165840 | tf_op jit(solution)/shard_map/all_gather | solution.py:10
  413.4 15.2 %copy.48 = f32[96,8,32,256]{3,2,1,0:T(8,128)S(1)} copy(f32[96,8,32,256]{3,1,2,0:T(8,128)} %bitcast.41) | data formatting | bytes 50331648
  428.6 5.8 %bitcast_reduce_fusion = f32[256,768]{0,1:T(8,128)S(1)} fusion(f32[96,8,32,256]{3,2,1,0:T(8,128)S(1)} %copy.48), kind=kLoop, calls=%fused_computation | loop fusion | flops 6094848 | bytes 25952256 | tf_op jit(solution)/shard_map/reduce_sum | solution.py:11
  436.6 1.3 fusion.8
  437.9 0.8 copy.54
  (42 shorter events, 4.1 us)
Async XLA Ops:
  7.2 230.1 %copy-start = (f32[256,256]{1,0:T(8,128)S(1)}, f32[256,256]{1,0:T(8,128)}, u32[]{:S(2)}) copy-start(f32[256,256]{1,0:T(8,128)} %param.15) | copy-start | bytes 786436
  7.2 4.6 %copy-start.6 = (f32[384,256]{1,0:T(8,128)S(1)}, f32[384,256]{1,0:T(8,128)}, u32[]{:S(2)}) copy-start(f32[384,256]{1,0:T(8,128)} %param.13) | copy-start | bytes 1179652
  7.2 4.7 %copy-start.7 = (f32[384,256]{1,0:T(8,128)S(1)}, f32[384,256]{1,0:T(8,128)}, u32[]{:S(2)}) copy-start(f32[384,256]{1,0:T(8,128)} %param.10) | copy-start | bytes 1179652
  7.2 37.2 %all-gather.4.cloned.1.call-start = ((), (), s32[]{:S(2)}) async-start(), calls=%async_computation.2 | async-start | bytes 3932160 | tf_op jit(solution)/shard_map/all_gather | solution.py:87
  13.0 221.7 %reduce-scatter.2.cloned.1.call-start = ((), (), s32[]{:S(2)}) async-start(), calls=%async_computation.3 | async-start | bytes 7077888 | tf_op jit(solution)/shard_map/reduce_scatter | solution.py:90
  66.5 1.1 copy-start.1
  66.6 174.0 %copy-start.8 = (s32[6,1]{0,1:T(1,128)S(1)}, s32[6,1]{0,1:T(1,128)}, u32[]{:S(2)}) copy-start(s32[6,1]{0,1:T(1,128)} %param.17) | copy-start | bytes 76
  66.6 346.8 %all-gather.6.cloned.1.call-start = ((), (), s32[]{:S(2)}) async-start(), calls=%async_computation.4 | async-start | bytes 25952256 | tf_op jit(solution)/shard_map/all_gather | solution.py:10
  67.7 168.1 %collective-permute-start = (f32[384,512]{1,0:T(8,128)S(1)}, f32[384,512]{1,0:T(8,128)S(1)}, u32[]{:S(2)}, u32[]{:S(2)}) collective-permute-start(f32[384,512]{1,0:T(8,128)S(1)} %copy-done.1), channel_id=1, source_target_pairs={{0,0},{1,4},{2,8},{3,12},{4,16},{5,20},{6,24},{7,28},{8,1},{9,5},{... | collective-permute-start | bytes 2359304 | tf_op jit(solution)/shard_map/ppermute | solution.py:89
  242.5 16.2 %all-to-all-start = ((f32[4,2,64,256]{3,2,1,0:T(8,128)}), f32[4,2,64,256]{3,2,1,0:T(8,128)S(1)}, u32[]{:S(2)}, u32[]{:S(2)}) async-start(f32[4,2,64,256]{3,2,1,0:T(8,128)} %copy.40), calls=%async_computation.1 | async-start | bytes 1048576 | tf_op jit(solution)/shard_map/all_to_all | solution.py:56
  428.6 6.3 %copy-start.2 = (f32[256,256]{1,0:T(8,128)S(1)}, f32[256,256]{1,0:T(8,128)}, u32[]{:S(2)}) copy-start(f32[256,256]{1,0:T(8,128)} %param.12) | copy-start | bytes 786436
  434.4 1.5 copy-start.3
  435.5 3.1 copy-start.4
  435.9 2.7 copy-start.5
Sparse Core Ops, SparseCore 0:
  13.2 31.2 all-gather.3
  66.7 168.0 reduce-scatter.1
  240.7 172.6 all-gather.5
